TPU v7x, 128 devices: a whole 4x4x4 slice. The times are simulated.
128 devices in a mesh: dp: 16 (over y, x), head: 8 (over z, core).
Axes of the slice: x: 4, y: 4, z: 4, core: 2. Of those that a mesh axis runs over, the one named last changes fastest.
Arguments:
- slot_token_ids: int32 [128, 512], P('dp'), may hold values from 0 to 50264
- lengths: int32 [128], P('dp'), may hold values from 64 to 512, as said below
- labels: int32 [128], P('dp'), may hold values from 0 to 2
- optimizer_step_count: int32 [], replicated, may hold values from 2 to 20
- token_embedding_table: bfloat16 [50304, 1024], P('dp', 'head'), may hold values from -6 to 6
- positions: bfloat16 [512, 1024], replicated, may hold values from -4 to 4
- query_key_value_weight: bfloat16 [3, 1024, 1024], P(None, None, 'head'), may hold values from -0.1875 to 0.1875
- attention_output_weight: bfloat16 [1024, 1024], P('head'), may hold values from -0.8 to 0.8
- feedforward_input_weight: bfloat16 [1024, 4096], P(None, 'head'), may hold values from -0.1875 to 0.1875
- feedforward_output_weight: bfloat16 [4096, 1024], P('head'), may hold values from -0.09375 to 0.09375
- layer_norm_gains: float32 [3, 1024], replicated, may hold values from 0.5 to 1.5
- layer_norm_biases: float32 [3, 1024], replicated, may hold values from -2 to 2
- classifier: bfloat16 [3, 1024], replicated, may hold values from -0.75 to 0.75
- adapter_down_maps: float32 [2, 1024, 16], replicated, may hold values from -0.1875 to 0.1875
- adapter_up_maps: float32 [2, 16, 1024], P(None, None, 'head'), may hold values from -1.5 to 1.5
- down_first_moment: float32 [2, 1024, 16], P(None, 'dp'), may hold values from -0.0078125 to 0.0078125
- down_second_moment: float32 [2, 1024, 16], P(None, 'dp'), may hold values from 2.1972657e-08 to 9.1552735e-08
- up_first_moment: float32 [2, 16, 1024], P(None, None, ('head', 'dp')), may hold values from -0.0078125 to 0.0078125
- up_second_moment: float32 [2, 16, 1024], P(None, None, ('head', 'dp')), may hold values from 2.1972657e-08 to 9.1552735e-08
- down_privacy_noise: float32 [2, 1024, 16], P(None, 'dp'), may hold values from -6 to 6
- up_privacy_noise: float32 [2, 16, 1024], P(None, None, ('head', 'dp')), may hold values from -6 to 6
Outputs:
- loss: float32 [], replicated
- example_norms: float32 [128], P(('dp', 'head'))
- a_moment1: float32 [2, 1024, 16], P(None, 'dp')
- a_moment2: float32 [2, 1024, 16], P(None, 'dp')
- a_weight: float32 [2, 1024, 16], P(None, 'dp')
- b_moment1: float32 [2, 16, 1024], P(None, None, ('head', 'dp'))
- b_moment2: float32 [2, 16, 1024], P(None, None, ('head', 'dp'))
- b_weight: float32 [2, 16, 1024], P(None, None, ('head', 'dp'))
- lamb_norms: float32 [4, 2], replicated
Inputs may be any that keep to these rules, and one draw needn't show every extreme that they name: `lengths`: valid tokens of each example; some example has exactly 512.
All inputs are finite; a program needn't handle non-finite values.
Results may differ from a plain program's by a relative error of at most 0.0059.
Values may be sent and summed in bfloat16 or wider, within the bound.
No kernel may reach another device: no remote copies, remote signals or barrier semaphores. Data moves between devices by JAX's collectives and lax.ppermute only.
A program may use at most 256 MiB of HBM per device.

v0:
```python
import jax
import jax.numpy as jnp
from jax import lax
from jax.sharding import PartitionSpec as P

HDIM = 64
MICRO = 4
precise = lax.Precision.HIGHEST
adapter_scale = 2.0
clip_bound = 1.0
noise_mult = 0.6
smooth_rate = 0.1
beta_one = 0.9
beta_two = 0.999
adam_eps = 1e-06
decay_rate = 0.01
learn_rate = 0.25
norm_eps = 1e-05
contract_last = (((1,), (1,)), ((), ()))


def gelu_exact(inputs):
    return jax.nn.gelu(inputs, approximate=False)


def norm_rows(inputs, gain, bias):
    centre = inputs - jnp.mean(inputs, -1, keepdims=True)
    inv_std = lax.rsqrt(jnp.mean(centre * centre, -1, keepdims=True) + norm_eps)
    return (centre * inv_std * gain + bias, inv_std)


def norm_back(grad, normed, inv_std, gain, bias):
    x_hat = (normed - bias) / gain
    scaled = grad * gain
    return inv_std * (
        scaled
        - jnp.mean(scaled, -1, keepdims=True)
        - x_hat * jnp.mean(scaled * x_hat, -1, keepdims=True)
    )


def branch_add(partial_out, resid, gain, bias):
    total = lax.psum(partial_out, "head")
    return norm_rows(resid + total, gain, bias)


def masked_scores(query_h, key_h, valid_mask):
    scores = jnp.einsum(
        "eqhd,ekhd->ehqk", query_h, key_h, preferred_element_type=jnp.float32
    ) * HDIM ** (-0.5)
    return jnp.where(valid_mask[:, None, None, :], scores, -1e30)


def layer_forward(
    hidden_initial, valid_mask, length_float, class_label, frozen_params, adapter_reduced
):
    w_qkv, w_o, w_in, w_out, gains, biases, class_w = frozen_params
    down_pair, up_reduced = adapter_reduced
    example_count, sequence_length = valid_mask.shape
    width = hidden_initial.shape[1]
    local_w = w_o.shape[0]
    adapter_width = up_reduced.shape[1]
    shape4 = (example_count, sequence_length, local_w // HDIM, HDIM)
    hidden_reduced = hidden_initial.astype(jnp.bfloat16)
    adapter_activation = jnp.dot(
        hidden_reduced, down_pair, preferred_element_type=jnp.float32
    ).astype(jnp.bfloat16)
    query_low = (
        (
            jnp.dot(hidden_reduced, w_qkv[0], preferred_element_type=jnp.float32)
            + adapter_scale
            * jnp.dot(
                adapter_activation[:, :adapter_width],
                up_reduced[0],
                preferred_element_type=jnp.float32,
            )
        )
        .astype(jnp.bfloat16)
        .reshape(shape4)
    )
    key_low = (
        jnp.dot(hidden_reduced, w_qkv[1], preferred_element_type=jnp.float32)
        .astype(jnp.bfloat16)
        .reshape(shape4)
    )
    value_low = (
        (
            jnp.dot(hidden_reduced, w_qkv[2], preferred_element_type=jnp.float32)
            + adapter_scale
            * jnp.dot(
                adapter_activation[:, adapter_width:],
                up_reduced[1],
                preferred_element_type=jnp.float32,
            )
        )
        .astype(jnp.bfloat16)
        .reshape(shape4)
    )
    scores = masked_scores(query_low, key_low, valid_mask)
    row_top = jnp.max(scores, -1, keepdims=True)
    log_total = row_top + jnp.log(jnp.sum(jnp.exp(scores - row_top), -1, keepdims=True))
    attn_prob = jnp.exp(scores - log_total)
    context = (
        jnp.einsum(
            "ehqk,ekhd->eqhd",
            attn_prob.astype(jnp.bfloat16),
            value_low,
            preferred_element_type=jnp.float32,
        )
        .astype(jnp.bfloat16)
        .reshape(-1, local_w)
    )
    hidden_one, std_one = branch_add(
        jnp.dot(context, w_o, preferred_element_type=jnp.float32),
        hidden_initial,
        gains[1],
        biases[1],
    )
    ffn_pre = jnp.dot(hidden_one.astype(jnp.bfloat16), w_in, preferred_element_type=jnp.float32)
    ffn_part = jnp.dot(
        gelu_exact(ffn_pre).astype(jnp.bfloat16), w_out, preferred_element_type=jnp.float32
    )
    hidden_two, std_two = branch_add(ffn_part, hidden_one, gains[2], biases[2])
    valid_f = valid_mask.astype(jnp.float32)
    pooled = (
        jnp.sum(hidden_two.reshape(example_count, sequence_length, width) * valid_f[..., None], 1)
        / length_float[:, None]
    )
    logits = lax.dot_general(
        pooled.astype(jnp.bfloat16), class_w, contract_last, preferred_element_type=jnp.float32
    )
    log_prob = jax.nn.log_softmax(logits, -1)
    target = (1.0 - smooth_rate) * jax.nn.one_hot(
        class_label, class_w.shape[0], dtype=jnp.float32
    ) + smooth_rate / class_w.shape[0]
    losses = -jnp.sum(target * log_prob, -1)
    d_logit = jnp.exp(log_prob) - target
    d_pooled = jnp.dot(d_logit, class_w.astype(jnp.float32), precision=precise)
    d_two = (d_pooled[:, None, :] * (valid_f / length_float[:, None])[..., None]).reshape(-1, width)
    d_sum_two = norm_back(d_two, hidden_two, std_two, gains[2], biases[2])
    grad_act = lax.dot_general(
        d_sum_two.astype(jnp.bfloat16), w_out, contract_last, preferred_element_type=jnp.float32
    )
    d_pre = jax.vjp(gelu_exact, ffn_pre)[1](grad_act)[0].astype(jnp.bfloat16)
    back_part = lax.dot_general(d_pre, w_in, contract_last, preferred_element_type=jnp.float32)
    d_one = d_sum_two + lax.psum(back_part, "head")
    d_attn = norm_back(d_one, hidden_one, std_one, gains[1], biases[1]).astype(jnp.bfloat16)
    d_context = (
        lax.dot_general(d_attn, w_o, contract_last, preferred_element_type=jnp.float32)
        .astype(jnp.bfloat16)
        .reshape(shape4)
    )
    attn_prob = jnp.exp(masked_scores(query_low, key_low, valid_mask) - log_total)
    d_value = jnp.einsum(
        "ehqk,eqhd->ekhd",
        attn_prob.astype(jnp.bfloat16),
        d_context,
        preferred_element_type=jnp.float32,
    ).astype(jnp.bfloat16)
    d_prob = jnp.einsum("eqhd,ekhd->ehqk", d_context, value_low, preferred_element_type=jnp.float32)
    d_score = (attn_prob * (d_prob - jnp.sum(attn_prob * d_prob, -1, keepdims=True))).astype(
        jnp.bfloat16
    )
    d_query = (
        jnp.einsum("ehqk,ekhd->eqhd", d_score, key_low, preferred_element_type=jnp.float32)
        * HDIM ** (-0.5)
    ).astype(jnp.bfloat16)
    dq_rows = d_query.reshape(-1, local_w)
    dv_rows = d_value.reshape(-1, local_w)
    example_activation = adapter_activation.reshape(
        example_count, sequence_length, 2 * adapter_width
    )
    up_gradient = adapter_scale * jnp.stack(
        [
            jnp.einsum(
                "elr,eld->erd",
                example_activation[..., :adapter_width],
                dq_rows.reshape(example_count, sequence_length, local_w),
                preferred_element_type=jnp.float32,
            ),
            jnp.einsum(
                "elr,eld->erd",
                example_activation[..., adapter_width:],
                dv_rows.reshape(example_count, sequence_length, local_w),
                preferred_element_type=jnp.float32,
            ),
        ],
        1,
    )
    inner_portion = adapter_scale * jnp.concatenate(
        [
            lax.dot_general(
                dq_rows, up_reduced[0], contract_last, preferred_element_type=jnp.float32
            ),
            lax.dot_general(
                dv_rows, up_reduced[1], contract_last, preferred_element_type=jnp.float32
            ),
        ],
        1,
    )
    inner_full = lax.psum(inner_portion, "head")
    inner_sum = inner_full.astype(jnp.bfloat16)
    grad_both = jnp.einsum(
        "eld,elr->edr",
        hidden_reduced.reshape(example_count, sequence_length, width),
        inner_sum.reshape(example_count, sequence_length, 2 * adapter_width),
        preferred_element_type=jnp.float32,
    )
    down_gradient = jnp.stack([grad_both[..., :adapter_width], grad_both[..., adapter_width:]], 1)
    return (losses, down_gradient, up_gradient)


def apply_blocks(hidden_rows, lengths, labels, frozen_params, adapter_reduced, encoder_block):
    example_count, sequence_length, width = hidden_rows.shape
    valid_all = jnp.arange(sequence_length)[None, :] < lengths[:, None]
    loss_list, down_list, up_list = ([], [], [])
    for block_idx in range(example_count // encoder_block):
        first_ex = block_idx * encoder_block
        last_ex = first_ex + encoder_block
        losses, down_gradient, up_gradient = layer_forward(
            hidden_rows[first_ex:last_ex].reshape(-1, width),
            valid_all[first_ex:last_ex],
            lengths[first_ex:last_ex].astype(jnp.float32),
            labels[first_ex:last_ex],
            frozen_params,
            adapter_reduced,
        )
        loss_list.append(losses)
        down_list.append(down_gradient)
        up_list.append(up_gradient)
    return (
        jnp.concatenate(loss_list, 0),
        jnp.concatenate(down_list, 0),
        jnp.concatenate(up_list, 0),
    )


def lamb_direction(weight, grad, first, second, step_number):
    first_new = beta_one * first + (1.0 - beta_one) * grad
    second_new = beta_two * second + (1.0 - beta_two) * grad * grad
    direction = (
        first_new
        / (1.0 - jnp.power(beta_one, step_number))
        / (jnp.sqrt(second_new / (1.0 - jnp.power(beta_two, step_number))) + adam_eps)
        + decay_rate * weight
    )
    return (first_new, second_new, direction)


def per_device(
    slot_token_ids,
    lengths,
    labels,
    optimizer_step_count,
    token_embedding_table,
    positions,
    query_key_value_weight,
    attention_output_weight,
    feedforward_input_weight,
    feedforward_output_weight,
    layer_norm_gains,
    layer_norm_biases,
    classifier,
    adapter_down_maps,
    adapter_up_maps,
    down_first_moment,
    down_second_moment,
    up_first_moment,
    up_second_moment,
    down_privacy_noise,
    up_privacy_noise,
):
    n_head = lax.axis_size("head")
    dataset_size = lax.axis_size("dp")
    ex_dev, sequence_length = slot_token_ids.shape
    width = positions.shape[1]
    every_ids = lax.all_gather(slot_token_ids, "dp", axis=0, tiled=True).reshape(-1)
    vocab_local = token_embedding_table.shape[0]
    offset = lax.axis_index("dp") * vocab_local
    ids_here = every_ids - offset
    inside = (ids_here >= 0) & (ids_here < vocab_local)
    picked = jnp.take(token_embedding_table, jnp.clip(ids_here, 0, vocab_local - 1), axis=0)
    columns = lax.psum_scatter(
        jnp.where(inside[:, None], picked.astype(jnp.float32), 0.0).astype(jnp.bfloat16),
        "dp",
        scatter_dimension=0,
        tiled=True,
    )
    pos_f = positions.astype(jnp.float32)[None]
    down_reduced = adapter_down_maps.astype(jnp.bfloat16)
    down_pair = jnp.concatenate([down_reduced[0], down_reduced[1]], 1)
    micro_examples = ex_dev // MICRO
    own_share = ex_dev // n_head
    tokens = lax.all_gather(columns, "head", axis=1, tiled=True)
    hidden_all, unused_std = norm_rows(
        tokens.astype(jnp.float32).reshape(ex_dev, sequence_length, width) + pos_f,
        layer_norm_gains[0],
        layer_norm_biases[0],
    )
    frozen_params = (
        query_key_value_weight,
        attention_output_weight,
        feedforward_input_weight,
        feedforward_output_weight,
        layer_norm_gains,
        layer_norm_biases,
        classifier,
    )
    losses, grads_down, grads_up = apply_blocks(
        hidden_all,
        lengths,
        labels,
        frozen_params,
        (down_pair, adapter_up_maps.astype(jnp.bfloat16)),
        micro_examples,
    )
    part_sums = jnp.sum(grads_down * grads_down, (1, 2, 3)) / n_head + jnp.sum(
        grads_up * grads_up, (1, 2, 3)
    )
    arrived = lax.all_to_all(
        part_sums.reshape(n_head, own_share), "head", split_axis=0, concat_axis=0, tiled=True
    )
    example_norms = jnp.sqrt(jnp.sum(arrived, 0))
    own_factor = clip_bound / jnp.maximum(example_norms, clip_bound)
    factors = lax.all_gather(own_factor, "head", axis=0, tiled=True)
    sum_down = jnp.einsum("e,eabc->abc", factors, grads_down, precision=precise)
    sum_up = jnp.einsum("e,eabc->abc", factors, grads_up, precision=precise)
    loss_part = jnp.sum(losses) / n_head
    red_down, red_up = (
        lax.psum_scatter(sum_down, "dp", scatter_dimension=1, tiled=True),
        lax.psum_scatter(sum_up, "dp", scatter_dimension=2, tiled=True),
    )
    examples = ex_dev * dataset_size
    down_gradient = (red_down + noise_mult * clip_bound * down_privacy_noise) / examples
    up_gradient = (red_up + noise_mult * clip_bound * up_privacy_noise) / examples
    step_number = optimizer_step_count.astype(jnp.float32)
    down_rows = adapter_down_maps.shape[1] // dataset_size
    down_weight = lax.dynamic_slice_in_dim(
        adapter_down_maps, lax.axis_index("dp") * down_rows, down_rows, 1
    )
    up_columns = adapter_up_maps.shape[2] // dataset_size
    up_weight = lax.dynamic_slice_in_dim(
        adapter_up_maps, lax.axis_index("dp") * up_columns, up_columns, 2
    )
    down_momentum, down_velocity, dir_down = lamb_direction(
        down_weight, down_gradient, down_first_moment, down_second_moment, step_number
    )
    up_momentum, up_velocity, dir_up = lamb_direction(
        up_weight, up_gradient, up_first_moment, up_second_moment, step_number
    )
    sq_down = (
        jnp.stack(
            [jnp.sum(down_weight * down_weight, (1, 2)), jnp.sum(dir_down * dir_down, (1, 2))], 1
        )
        / n_head
    )
    sq_up = jnp.stack([jnp.sum(up_weight * up_weight, (1, 2)), jnp.sum(dir_up * dir_up, (1, 2))], 1)
    total_down, total_up, loss_sum = lax.psum((sq_down, sq_up, loss_part), ("dp", "head"))
    norm_table = jnp.sqrt(jnp.concatenate([total_down, total_up], 0))
    updated_down = (
        down_weight - learn_rate * (norm_table[:2, 0] / norm_table[:2, 1])[:, None, None] * dir_down
    )
    updated_up = (
        up_weight - learn_rate * (norm_table[2:, 0] / norm_table[2:, 1])[:, None, None] * dir_up
    )
    return (
        loss_sum / examples,
        example_norms,
        down_momentum,
        down_velocity,
        updated_down,
        up_momentum,
        up_velocity,
        updated_up,
        norm_table,
    )


def solution(mesh):
    placed = (
        P("dp", None),
        P("dp"),
        P("dp"),
        P(),
        P("dp", "head"),
        P(),
        P(None, None, "head"),
        P("head", None),
        P(None, "head"),
        P("head", None),
        P(),
        P(),
        P(),
        P(),
        P(None, None, "head"),
        P(None, "dp", None),
        P(None, "dp", None),
        P(None, None, ("head", "dp")),
        P(None, None, ("head", "dp")),
        P(None, "dp", None),
        P(None, None, ("head", "dp")),
    )
    return jax.shard_map(
        per_device,
        mesh=mesh,
        in_specs=placed,
        out_specs=(
            P(),
            P(("dp", "head")),
            P(None, "dp", None),
            P(None, "dp", None),
            P(None, "dp", None),
            P(None, None, ("head", "dp")),
            P(None, None, ("head", "dp")),
            P(None, None, ("head", "dp")),
            P(),
        ),
        check_vma=False,
    )
```

profile of v0, /device:TPU:1, one launch (start us, length us, event | category | flops | bytes accessed | tf_op | source)
XLA Modules:
  0.0 1647.0 jit_solution(5846328891770936799)
XLA Ops:
  7.3 19.8 %all_gather.9 = s32[128,512]{1,0:T(8,128)S(1)} all-gather(s32[8,512]{1,0:T(8,128)} %param.22), channel_id=1, replica_groups=mesh['dp'=16,'head'=8] {'dp'}, dimensions={0}, use_global_device_ids=true | all-gather | bytes 278528 | tf_op jit(solution)/shard_map/all_gather | solution.py:277
  28.1 229.0 %gather_fusion = bf16[65536,128]{1,0:T(8,128)(2,1)} fusion(bf16[3144,128]{1,0:T(8,128)(2,1)S(1)} %copy-done.1, s32[65536]{0:T(1024)S(1)} %broadcast_clamp_fusion), kind=kCustom, calls=%fused_computation | custom fusion | bytes 33816576 | tf_op jit(solution)/shard_map/jit(_take)/gather | solution.py:282
  257.0 46.3 %select_convert_fusion = bf16[65536,128]{1,0:T(8,128)(2,1)} fusion(bf16[65536,128]{1,0:T(8,128)(2,1)} %gather_fusion, pred[65536]{0:T(1024)(128)(4,1)S(1)} %compare_and_fusion, pred[65536]{0:T(1024)(128)(4,1)S(1)} %bitcast.555), kind=kLoop, calls=%fused_computation.1 | loop fusion | flops 33554432 | bytes 33685504 | tf_op jit(solution)/shard_map/convert_element_type | solution.py:284
  303.4 115.6 %reduce-scatter.6.cloned.1.call-done = bf16[4096,128]{1,0:T(8,128)(2,1)} async-done(((bf16[65536,128]{1,0:T(8,128)(2,1)}), bf16[4096,128]{1,0:T(8,128)(2,1)}) %reduce-scatter.6.cloned.1.call-update) | async-done | bytes 1048592 | tf_op jit(solution)/shard_map/reduce_scatter | solution.py:283
  423.8 51.6 %all-gather.2.cloned.1.call-done = bf16[4096,1024]{1,0:T(8,128)(2,1)} async-done(((bf16[4096,128]{1,0:T(8,128)(2,1)}), bf16[4096,1024]{1,0:T(8,128)(2,1)}) %all-gather.2.cloned.1.call-update) | async-done | bytes 8388624 | tf_op jit(solution)/shard_map/all_gather | solution.py:294
  475.4 5.1 fusion
  480.5 5.9 multiply_reduce_fusion
  486.4 6.1 multiply_add_fusion
  492.5 3.6 fusion.384
  496.1 4.8 fusion.383
  501.0 3.9 fusion.183
  527.2 2.6 bitcast_convert_fusion.1
  535.6 1.9 exponential_reduce_fusion
  547.3 2.6 bitcast_convert_fusion.3
  555.7 2.3 exponential_reduce_fusion.2
  559.6 2.7 fusion.407
  562.2 2.7 fusion.405
  565.9 3.3 fusion.135
  569.6 2.8 fusion.406
  574.0 3.3 fusion.133
  577.5 2.7 fusion.404
  580.3 183.9 %all-reduce.15.cloned.1.call-done = (f32[1024,1024]{1,0:T(8,128)}, f32[1024,1024]{1,0:T(8,128)}, f32[1024,1024]{1,0:T(8,128)}, f32[1024,1024]{1,0:T(8,128)}) async-done(((f32[1024,1024]{1,0:T(8,128)}, f32[1024,1024]{1,0:T(8,128)}, f32[1024,1024]{1,0:T(8,128)}, f32[1024,1024]{1,0:T(8,128)}), (f32[1024,1024]{1,0:T(8,128)}, f32[1024,1024]{1,0:T(8,128)}, f32[1024,1024]{1,0:T(8,128)}, ...) | async-done | bytes 16777232 | tf_op jit(solution)/shard_map/psum | solution.py:43
  764.3 4.1 fusion.382
  769.0 3.2 copy-done.31
  777.6 6.8 fusion.140
  784.4 6.7 fusion.138
  794.9 6.7 fusion.139
  806.8 6.7 fusion.137
  814.4 183.4 %all-reduce.13.cloned.1.call-done = (f32[1024,1024]{1,0:T(8,128)}, f32[1024,1024]{1,0:T(8,128)}, f32[1024,1024]{1,0:T(8,128)}, f32[1024,1024]{1,0:T(8,128)}) async-done(((f32[1024,1024]{1,0:T(8,128)}, f32[1024,1024]{1,0:T(8,128)}, f32[1024,1024]{1,0:T(8,128)}, f32[1024,1024]{1,0:T(8,128)}), (f32[1024,1024]{1,0:T(8,128)}, f32[1024,1024]{1,0:T(8,128)}, f32[1024,1024]{1,0:T(8,128)}, ...) | async-done | bytes 16777232 | tf_op jit(solution)/shard_map/psum | solution.py:43
  997.8 12.3 fusion.371
  1012.7 4.3 multiply_reduce_fusion.13
  1019.7 5.7 fusion.24
  1025.7 2.0 multiply_reduce_fusion.12
  1027.7 8.9 fusion.18
  1036.7 10.9 fusion.144
  1047.5 3.9 fusion.31
  1051.4 11.0 fusion.143
  1062.5 7.4 fusion.29
  1069.8 10.8 fusion.142
  1080.6 10.9 fusion.141
  1102.5 173.5 %all-reduce.11.cloned.1.call-done = (f32[1024,1024]{1,0:T(8,128)}, f32[1024,1024]{1,0:T(8,128)}, f32[1024,1024]{1,0:T(8,128)}, f32[1024,1024]{1,0:T(8,128)}) async-done(((f32[1024,1024]{1,0:T(8,128)}, f32[1024,1024]{1,0:T(8,128)}, f32[1024,1024]{1,0:T(8,128)}, f32[1024,1024]{1,0:T(8,128)}), (f32[1024,1024]{1,0:T(8,128)}, f32[1024,1024]{1,0:T(8,128)}, f32[1024,1024]{1,0:T(8,128)}, ...) | async-done | bytes 16777232 | tf_op jit(solution)/shard_map/psum | solution.py:146
  1276.0 7.9 fusion.370
  1283.9 2.1 fusion.121
  1286.7 3.5 convolution_convert_fusion
  1290.3 2.9 multiply_reduce_fusion.1
  1295.3 5.9 fusion.369
  1301.2 2.1 fusion.122
  1304.0 3.5 convolution_convert_fusion.1
  1307.6 3.5 multiply_reduce_fusion.4
  1312.6 5.9 fusion.368
  1318.6 2.1 fusion.123
  1321.4 3.5 convolution_convert_fusion.2
  1324.9 3.6 multiply_reduce_fusion.7
  1330.0 5.9 fusion.367
  1335.9 2.1 fusion.124
  1338.7 3.5 convolution_convert_fusion.3
  1356.5 1.7 fusion.117
  1359.7 29.7 %all-reduce.16 = (bf16[1024,32]{0,1:T(8,128)(2,1)}, bf16[1024,32]{0,1:T(8,128)(2,1)}, bf16[1024,32]{0,1:T(8,128)(2,1)}, bf16[1024,32]{0,1:T(8,128)(2,1)}) all-reduce(f32[1024,32]{0,1:T(8,128)S(1)} %maximum_multiply_fusion.3, f32[1024,32]{0,1:T(8,128)} %maximum_multiply_fusion.2, ...), channel_id=1, replica_groups=mesh['dp'=16,'head'=8] {'head'}, use_global_device_ids=true, to_apply=%region_73.75 | all-reduce | flops 131072 | bytes 786432 | tf_op jit(solution)/shard_map/psum | solution.py:201
  1389.5 2.1 fusion.205
  1396.8 10.8 all_to_all.6
  1409.6 12.5 all-reduce
  1426.7 64.2 %reduce-scatter.8.cloned.1.call-done = f32[2,16,8]{1,2,0:T(8,128)} async-done(((f32[2,16,128]{1,2,0:T(8,128)}), f32[2,16,8]{1,2,0:T(8,128)}) %reduce-scatter.8.cloned.1.call-update) | async-done | bytes 1040 | tf_op jit(solution)/shard_map/reduce_scatter | solution.py:331
  1492.3 74.0 %reduce-scatter.10.cloned.1.call-done = f32[64,32]{1,0:T(8,128)} async-done(((f32[1024,32]{1,0:T(8,128)}), f32[64,32]{1,0:T(8,128)}) %reduce-scatter.10.cloned.1.call-update) | async-done | bytes 8208
  1568.7 66.1 %all-reduce.1 = (f32[]{:T(128)}, f32[2,2]{0,1:T(2,128)S(1)}, f32[2,2]{0,1:T(2,128)S(1)}) all-reduce(f32[]{:T(128)S(6)} %div.320, f32[2,2]{0,1:T(2,128)S(1)} %pad_maximum_fusion.2, f32[2,2]{0,1:T(2,128)S(1)} %maximum_multiply_fusion.8), channel_id=1, replica_groups=mesh['dp'=16,'head'=8] {'dp','head'}, use_global_device_ids=true, to_apply=%region_45.47 | all-reduce | flops 9 | bytes 72 | tf_op jit(solution)/shard_map/psum | solution.py:358
  (595 shorter events, 122.0 us)
Async XLA Ops:
  7.2 770.4 %copy-start = (bf16[512,1024]{1,0:T(8,128)(2,1)S(1)}, bf16[512,1024]{1,0:T(8,128)(2,1)}, u32[]{:S(2)}) copy-start(bf16[512,1024]{1,0:T(8,128)(2,1)} %param.31) | copy-start | bytes 3145732
  7.2 20.9 %copy-start.1 = (bf16[3144,128]{1,0:T(8,128)(2,1)S(1)}, bf16[3144,128]{1,0:T(8,128)(2,1)}, u32[]{:S(2)}) copy-start(bf16[3144,128]{1,0:T(8,128)(2,1)} %param.26) | copy-start | bytes 2414596
  7.2 411.8 %reduce-scatter.6.cloned.1.call-start = ((), (), s32[]{:S(2)}) async-start(), calls=%async_computation.4 | async-start | bytes 17825792 | tf_op jit(solution)/shard_map/reduce_scatter | solution.py:283
  303.3 172.0 %all-gather.2.cloned.1.call-start = ((), (), s32[]{:S(2)}) async-start(), calls=%async_computation.5 | async-start | bytes 9437184 | tf_op jit(solution)/shard_map/all_gather | solution.py:294
  419.0 3.5 copy-start.151
  419.0 345.2 %all-reduce.15.cloned.1.call-start = ((), (), s32[]{:S(2)}) async-start(), calls=%async_computation.10 | async-start | bytes 33554432 | tf_op jit(solution)/shard_map/psum | solution.py:43
  420.7 151.7 %copy-start.88 = (bf16[2,16,128]{2,1,0:T(8,128)(2,1)}, bf16[2,16,128]{2,1,0:T(8,128)(2,1)S(1)}, u32[]{:S(2)}) copy-start(bf16[2,16,128]{2,1,0:T(8,128)(2,1)S(1)} %convert_element_type.351) | copy-start | bytes 24580
  422.0 151.4 %copy-start.111 = (pred[2,512]{1,0:T(4,128)(4,1)}, pred[2,512]{1,0:T(4,128)(4,1)S(1)}, u32[]{:S(2)}) copy-start(pred[2,512]{1,0:T(4,128)(4,1)S(1)} %get-tuple-element.137) | copy-start | bytes 3076
  500.9 19.8 %copy-start.32 = (f32[2,512,1024]{2,1,0:T(8,128)}, f32[2,512,1024]{2,1,0:T(8,128)S(1)}, u32[]{:S(2)}) copy-start(f32[2,512,1024]{2,1,0:T(8,128)S(1)} %get-tuple-element.79) | copy-start | bytes 12582916
  500.9 3.9 copy-start.39
  501.0 4.0 copy-start.43
  523.1 14.8 copy-start.71
  524.8 8.6 copy-start.53
  527.2 7.3 copy-start.49
  529.9 3.6 copy-start.118
  542.7 15.3 copy-start.69
  544.4 9.1 copy-start.55
  547.3 7.3 copy-start.51
  550.0 3.6 copy-start.113
  573.3 3.9 copy-start.73
  580.3 417.5 %all-reduce.13.cloned.1.call-start = ((), (), s32[]{:S(2)}) async-start(), calls=%async_computation.9 | async-start | bytes 33554432 | tf_op jit(solution)/shard_map/psum | solution.py:43
  764.3 4.7 copy-start.48
  768.4 5.0 copy-start.26
  768.4 3.8 copy-start.31
  777.5 6.8 copy-start.160
  784.4 6.7 copy-start.29
  784.4 6.7 copy-start.47
  794.9 6.7 copy-start.163
  794.9 6.7 copy-start.28
  794.9 6.7 copy-start.46
  813.5 462.4 %all-reduce.11.cloned.1.call-start = ((), (), s32[]{:S(2)}) async-start(), calls=%async_computation.8 | async-start | bytes 33554432 | tf_op jit(solution)/shard_map/psum | solution.py:146
  1010.1 9.6 copy-start.2
  1010.1 9.6 copy-start.6
  1010.1 17.6 %copy-start.4 = (f32[1024,1024]{1,0:T(8,128)}, f32[1024,1024]{1,0:T(8,128)S(1)}, u32[]{:S(2)}) copy-start(f32[1024,1024]{1,0:T(8,128)S(1)} %get-tuple-element.121) | copy-start | bytes 12582916
  1010.1 17.6 %copy-start.8 = (f32[1024,1024]{1,0:T(8,128)}, f32[1024,1024]{1,0:T(8,128)S(1)}, u32[]{:S(2)}) copy-start(f32[1024,1024]{1,0:T(8,128)S(1)} %get-tuple-element.125) | copy-start | bytes 12582916
  1012.7 4.3 copy-start.158
  1091.6 399.3 %reduce-scatter.8.cloned.1.call-start = ((), (), s32[]{:S(2)}) async-start(), calls=%async_computation.6 | async-start | bytes 139264 | tf_op jit(solution)/shard_map/reduce_scatter | solution.py:331
  1275.9 7.9 copy-start.27
  1276.0 7.9 copy-start.45
  1286.7 3.5 copy-start.15
  1286.7 3.5 copy-start.72
  1290.2 53.7 %copy-start.78 = (bf16[2,2,64,512]{3,2,1,0:T(8,128)(2,1)}, bf16[2,2,64,512]{3,2,1,0:T(8,128)(2,1)S(1)}, u32[]{:S(2)}) copy-start(bf16[2,2,64,512]{3,2,1,0:T(8,128)(2,1)S(1)} %convolution_convert_fusion) | copy-start | bytes 786436
  1290.2 3.7 copy-start.7
  1290.2 5.0 copy-start.25
  1307.6 40.5 %copy-start.80 = (bf16[2,2,64,512]{3,2,1,0:T(8,128)(2,1)}, bf16[2,2,64,512]{3,2,1,0:T(8,128)(2,1)S(1)}, u32[]{:S(2)}) copy-start(bf16[2,2,64,512]{3,2,1,0:T(8,128)(2,1)S(1)} %convolution_convert_fusion.1) | copy-start | bytes 786436
  1307.6 3.7 copy-start.5
  1307.6 5.1 copy-start.23
  1324.9 27.4 %copy-start.82 = (bf16[2,2,64,512]{3,2,1,0:T(8,128)(2,1)}, bf16[2,2,64,512]{3,2,1,0:T(8,128)(2,1)S(1)}, u32[]{:S(2)}) copy-start(bf16[2,2,64,512]{3,2,1,0:T(8,128)(2,1)S(1)} %convolution_convert_fusion.2) | copy-start | bytes 786436
  1324.9 3.7 copy-start.3
  1324.9 5.1 copy-start.21
  1342.2 13.8 copy-start.84
  1342.3 3.5 copy-start.40
  1342.3 3.5 copy-start.54
  1349.4 3.6 copy-start.42
  1351.1 3.7 copy-start.57
  1358.9 32.7 %copy-start.38 = (bf16[2,512,1024]{2,1,0:T(8,128)(2,1)S(1)}, bf16[2,512,1024]{2,1,0:T(8,128)(2,1)}, u32[]{:S(2)}) copy-start(bf16[2,512,1024]{2,1,0:T(8,128)(2,1)} %get-tuple-element.84) | copy-start | bytes 6291460
  1423.1 143.2 %reduce-scatter.10.cloned.1.call-start = ((), (), s32[]{:S(2)}) async-start(), calls=%async_computation.7 | async-start | bytes 557056
  1423.2 67.7 %copy-start.122 = (f32[2,16,8]{1,2,0:T(8,128)S(1)}, f32[2,16,8]{1,2,0:T(8,128)}, u32[]{:S(2)}) copy-start(f32[2,16,8]{1,2,0:T(8,128)} %copy.338) | copy-start | bytes 3076
  1423.2 67.7 %copy-start.153 = (f32[2,16,8]{1,2,0:T(8,128)S(1)}, f32[2,16,8]{1,2,0:T(8,128)}, u32[]{:S(2)}) copy-start(f32[2,16,8]{1,2,0:T(8,128)} %param.42) | copy-start | bytes 3076
  1423.2 67.7 %copy-start.154 = (f32[2,16,8]{1,2,0:T(8,128)S(1)}, f32[2,16,8]{1,2,0:T(8,128)}, u32[]{:S(2)}) copy-start(f32[2,16,8]{1,2,0:T(8,128)} %param.40) | copy-start | bytes 3076
  1423.2 67.7 %copy-start.155 = (f32[2,16,8]{1,2,0:T(8,128)S(1)}, f32[2,16,8]{1,2,0:T(8,128)}, u32[]{:S(2)}) copy-start(f32[2,16,8]{1,2,0:T(8,128)} %param.39) | copy-start | bytes 3076
  1424.7 142.5 %copy-start.145 = (f32[2,64,16]{1,2,0:T(8,128)S(1)}, f32[2,64,16]{1,2,0:T(8,128)}, u32[]{:S(2)}) copy-start(f32[2,64,16]{1,2,0:T(8,128)} %param.41) | copy-start | bytes 24580
  1424.7 142.5 %copy-start.146 = (f32[2,64,16]{1,2,0:T(8,128)S(1)}, f32[2,64,16]{1,2,0:T(8,128)}, u32[]{:S(2)}) copy-start(f32[2,64,16]{1,2,0:T(8,128)} %param.38) | copy-start | bytes 24580
  1424.7 142.5 %copy-start.147 = (f32[2,64,16]{1,2,0:T(8,128)S(1)}, f32[2,64,16]{1,2,0:T(8,128)}, u32[]{:S(2)}) copy-start(f32[2,64,16]{1,2,0:T(8,128)} %param.37) | copy-start | bytes 24580
  (107 other events, 212.7 us)
Sparse Core Ops, SparseCore 0:
  303.4 115.5 reduce-scatter.5
  420.7 54.6 all-gather.1
  580.4 183.7 all-reduce.14
  813.6 184.1 all-reduce.12
  1091.7 184.2 all-reduce.10
  1423.2 67.6 reduce-scatter.7
  1494.4 71.8 reduce-scatter.9
where the time goes:
time: 1650 us
  waiting for transfers between devices  846 us (51%)
  local copies, waits for them, and re-layouts  291 us (18%)
  matrix products  177 us (11%)
  other arithmetic  169 us (10%)
  blocking collectives  139 us (8%)
  between operations  24.4 us (1%)
    psum x2, waiting for transfers between devices, branch_add(): total = lax.psum(partial_out, 'head')  367 us
    gather x1, local copies, waits for them, and re-layouts, per_device(): jnp.take(token_embedding_table, jnp.clip(ids_here, 0, vocab_local - 1), a...  229 us
    psum x1, waiting for transfers between devices, layer_forward(): d_one = d_sum_two + lax.psum(back_part, 'head')  173 us
    reduce_scatter x1, waiting for transfers between devices, per_device(): lax.psum_scatter(jnp.where(inside[:, None], picked.astype(jnp.float32), 0...  116 us
    unnamed x8, waiting for transfers between devices  74.1 us
    psum x1, blocking collectives, per_device(): lax.psum((sq_down, sq_up, loss_part), ('dp', 'head'))  66.1 us
    reduce_scatter x1, waiting for transfers between devices, per_device(): lax.psum_scatter(sum_up, 'dp', scatter_dimension=2, tiled=True)  64.2 us
    all_gather x1, waiting for transfers between devices, per_device(): tokens = lax.all_gather(columns, 'head', axis=1, tiled=True)  51.6 us
  transfers between devices with their start and end apart: 7, of which 7 were waited for; matrix products, arithmetic and copies ran while one was open for 1% of the time, Pallas kernels for 0%

commit v1 on v0

--- a/solution.py
+++ b/solution.py
@@ -40,7 +40,9 @@
 
 
 def branch_add(partial_out, resid, gain, bias):
-    total = lax.psum(partial_out, "head")
+    total = partial_out
+    for hop in (1, 2, 4):
+        total = total + lax.ppermute(total, "head", [(dev, dev ^ hop) for dev in range(8)])
     return norm_rows(resid + total, gain, bias)
 
 

time: 1650 us -> 2710 us (1.64)
  waiting for transfers between devices: 846 us -> 1800 us
  other arithmetic: 169 us -> 245 us
  starting transfers between devices: 0.29 us -> 30.8 us
    ppermute x0 -> x24, waiting for transfers between devices: none -> 1330 us  [branch_add(): lax.ppermute(total, 'head', [(dev, dev ^ hop) for dev in range(8)])]
    psum x2 -> x0, waiting for transfers between devices: 367 us -> none  [branch_add(): total = lax.psum(partial_out, 'head')]
    add x0 -> x16, other arithmetic: none -> 54.2 us  [branch_add(): total + lax.ppermute(total, 'head', [(dev, dev ^ hop) for dev in range(8)])]
    ppermute x0 -> x24, starting transfers between devices: none -> 30.6 us  [branch_add(): lax.ppermute(total, 'head', [(dev, dev ^ hop) for dev in range(8)])]
    unnamed x8 -> x6, waiting for transfers between devices: 74.1 us -> 73.9 us
  transfers between devices with their start and end apart: 7 -> 29, of which waited for: 7 -> 21; matrix products, arithmetic and copies ran while one was open for 1% -> 6% of each run, Pallas kernels for 0% -> 0%
where the time goes in v1:
time: 2710 us
  waiting for transfers between devices  1800 us (66%)
  local copies, waits for them, and re-layouts  290 us (11%)
  other arithmetic  245 us (9%)
  matrix products  172 us (6%)
  blocking collectives  139 us (5%)
  starting transfers between devices  30.8 us (1%)
    ppermute x24, waiting for transfers between devices, branch_add(): lax.ppermute(total, 'head', [(dev, dev ^ hop) for dev in range(8)])  1330 us
    gather x1, local copies, waits for them, and re-layouts, per_device(): jnp.take(token_embedding_table, jnp.clip(ids_here, 0, vocab_local - 1), a...  227 us
    psum x1, waiting for transfers between devices, layer_forward(): d_one = d_sum_two + lax.psum(back_part, 'head')  173 us
    reduce_scatter x1, waiting for transfers between devices, per_device(): lax.psum_scatter(jnp.where(inside[:, None], picked.astype(jnp.float32), 0...  116 us
    unnamed x6, waiting for transfers between devices  73.9 us
    psum x1, blocking collectives, per_device(): lax.psum((sq_down, sq_up, loss_part), ('dp', 'head'))  66.1 us
    reduce_scatter x1, waiting for transfers between devices, per_device(): lax.psum_scatter(sum_up, 'dp', scatter_dimension=2, tiled=True)  64.2 us
  transfers between devices with their start and end apart: 29, of which 21 were waited for; matrix products, arithmetic and copies ran while one was open for 6% of the time, Pallas kernels for 0%

profile of v1, /device:TPU:1, one launch (start us, length us, event | category | flops | bytes accessed | tf_op | source)
XLA Modules:
  0.0 2705.8 jit_solution(3901800284213158565)
XLA Ops:
  7.3 19.8 all_gather.9
  28.1 227.3 %gather_fusion = bf16[65536,128]{1,0:T(8,128)(2,1)} fusion(bf16[3144,128]{1,0:T(8,128)(2,1)S(1)} %copy-done.1, s32[65536]{0:T(1024)S(1)} %broadcast_clamp_fusion), kind=kCustom, calls=%fused_computation | custom fusion | bytes 33816576 | tf_op jit(solution)/shard_map/jit(_take)/gather | solution.py:284
  255.4 46.2 %select_convert_fusion = bf16[65536,128]{1,0:T(8,128)(2,1)} fusion(bf16[65536,128]{1,0:T(8,128)(2,1)} %gather_fusion, pred[65536]{0:T(1024)(128)(4,1)S(1)} %compare_and_fusion, pred[65536]{0:T(1024)(128)(4,1)S(1)} %bitcast.555), kind=kLoop, calls=%fused_computation.1 | loop fusion | flops 33554432 | bytes 33685504 | tf_op jit(solution)/shard_map/convert_element_type | solution.py:286
  301.7 115.8 %reduce-scatter.6.cloned.1.call-done = bf16[4096,128]{1,0:T(8,128)(2,1)} async-done(((bf16[65536,128]{1,0:T(8,128)(2,1)}), bf16[4096,128]{1,0:T(8,128)(2,1)}) %reduce-scatter.6.cloned.1.call-update) | async-done | bytes 1048592 | tf_op jit(solution)/shard_map/reduce_scatter | solution.py:285
  422.2 51.5 %all-gather.2.cloned.1.call-done = bf16[4096,1024]{1,0:T(8,128)(2,1)} async-done(((bf16[4096,128]{1,0:T(8,128)(2,1)}), bf16[4096,1024]{1,0:T(8,128)(2,1)}) %all-gather.2.cloned.1.call-update) | async-done | bytes 8388624 | tf_op jit(solution)/shard_map/all_gather | solution.py:296
  473.7 5.1 fusion
  478.8 5.9 multiply_reduce_fusion
  484.7 6.1 multiply_add_fusion
  490.8 3.6 fusion.376
  494.4 4.8 fusion.375
  499.2 3.9 fusion.179
  577.8 4.4 add.500
  583.4 4.4 add.448
  588.3 4.4 add.468
  595.4 78.8 %collective-permute-done.19 = f32[1024,1024]{1,0:T(8,128)S(1)} collective-permute-done((f32[1024,1024]{1,0:T(8,128)S(1)}, f32[1024,1024]{1,0:T(8,128)S(1)}, u32[]{:S(2)}, u32[]{:S(2)}) %collective-permute-start.19) | collective-permute-done | bytes 4194336 | tf_op jit(solution)/shard_map/ppermute | solution.py:45
  677.6 86.6 %collective-permute-done.1 = f32[1024,1024]{1,0:T(8,128)} collective-permute-done((f32[1024,1024]{1,0:T(8,128)S(1)}, f32[1024,1024]{1,0:T(8,128)}, u32[]{:S(2)}, u32[]{:S(2)}) %collective-permute-start.1) | collective-permute-done | bytes 4194336 | tf_op jit(solution)/shard_map/ppermute | solution.py:45
  764.2 5.2 add.449
  771.8 82.3 %collective-permute-done.7 = f32[1024,1024]{1,0:T(8,128)} collective-permute-done((f32[1024,1024]{1,0:T(8,128)S(1)}, f32[1024,1024]{1,0:T(8,128)}, u32[]{:S(2)}, u32[]{:S(2)}) %collective-permute-start.7) | collective-permute-done | bytes 4194336 | tf_op jit(solution)/shard_map/ppermute | solution.py:45
  859.7 84.3 %collective-permute-done.13 = f32[1024,1024]{1,0:T(8,128)} collective-permute-done((f32[1024,1024]{1,0:T(8,128)S(1)}, f32[1024,1024]{1,0:T(8,128)}, u32[]{:S(2)}, u32[]{:S(2)}) %collective-permute-start.13) | collective-permute-done | bytes 4194336 | tf_op jit(solution)/shard_map/ppermute | solution.py:45
  949.7 85.6 %collective-permute-done.20 = f32[1024,1024]{1,0:T(8,128)} collective-permute-done((f32[1024,1024]{1,0:T(8,128)S(1)}, f32[1024,1024]{1,0:T(8,128)}, u32[]{:S(2)}, u32[]{:S(2)}) %collective-permute-start.20) | collective-permute-done | bytes 4194336 | tf_op jit(solution)/shard_map/ppermute | solution.py:45
  1041.9 6.7 fusion.136
  1050.5 74.6 %collective-permute-done.2 = f32[1024,1024]{1,0:T(8,128)} collective-permute-done((f32[1024,1024]{1,0:T(8,128)}, f32[1024,1024]{1,0:T(8,128)}, u32[]{:S(2)}, u32[]{:S(2)}) %collective-permute-start.2) | collective-permute-done | bytes 4194336 | tf_op jit(solution)/shard_map/ppermute | solution.py:45
  1125.1 4.1 fusion.368
  1132.7 6.7 fusion.133
  1141.1 74.0 %collective-permute-done.8 = f32[1024,1024]{1,0:T(8,128)} collective-permute-done((f32[1024,1024]{1,0:T(8,128)S(1)}, f32[1024,1024]{1,0:T(8,128)}, u32[]{:S(2)}, u32[]{:S(2)}) %collective-permute-start.8) | collective-permute-done | bytes 4194336 | tf_op jit(solution)/shard_map/ppermute | solution.py:45
  1221.6 5.3 fusion.134
  1229.1 75.8 %collective-permute-done.14 = f32[1024,1024]{1,0:T(8,128)} collective-permute-done((f32[1024,1024]{1,0:T(8,128)S(1)}, f32[1024,1024]{1,0:T(8,128)}, u32[]{:S(2)}, u32[]{:S(2)}) %collective-permute-start.14) | collective-permute-done | bytes 4194336 | tf_op jit(solution)/shard_map/ppermute | solution.py:45
  1311.5 5.3 fusion.135
  1317.9 4.4 add.506
  1322.8 4.4 add.456
  1336.4 78.3 %collective-permute-done.22 = f32[1024,1024]{1,0:T(8,128)} collective-permute-done((f32[1024,1024]{1,0:T(8,128)S(1)}, f32[1024,1024]{1,0:T(8,128)}, u32[]{:S(2)}, u32[]{:S(2)}) %collective-permute-start.22) | collective-permute-done | bytes 4194336 | tf_op jit(solution)/shard_map/ppermute | solution.py:45
  1419.1 85.4 %collective-permute-done.4 = f32[1024,1024]{1,0:T(8,128)} collective-permute-done((f32[1024,1024]{1,0:T(8,128)S(1)}, f32[1024,1024]{1,0:T(8,128)}, u32[]{:S(2)}, u32[]{:S(2)}) %collective-permute-start.4) | collective-permute-done | bytes 4194336 | tf_op jit(solution)/shard_map/ppermute | solution.py:45
  1509.0 85.4 %collective-permute-done.10 = f32[1024,1024]{1,0:T(8,128)} collective-permute-done((f32[1024,1024]{1,0:T(8,128)S(1)}, f32[1024,1024]{1,0:T(8,128)}, u32[]{:S(2)}, u32[]{:S(2)}) %collective-permute-start.10) | collective-permute-done | bytes 4194336 | tf_op jit(solution)/shard_map/ppermute | solution.py:45
  1599.0 85.4 %collective-permute-done.16 = f32[1024,1024]{1,0:T(8,128)} collective-permute-done((f32[1024,1024]{1,0:T(8,128)S(1)}, f32[1024,1024]{1,0:T(8,128)}, u32[]{:S(2)}, u32[]{:S(2)}) %collective-permute-start.16) | collective-permute-done | bytes 4194336 | tf_op jit(solution)/shard_map/ppermute | solution.py:45
  1689.3 85.7 %collective-permute-done.23 = f32[1024,1024]{1,0:T(8,128)} collective-permute-done((f32[1024,1024]{1,0:T(8,128)S(1)}, f32[1024,1024]{1,0:T(8,128)}, u32[]{:S(2)}, u32[]{:S(2)}) %collective-permute-start.23) | collective-permute-done | bytes 4194336 | tf_op jit(solution)/shard_map/ppermute | solution.py:45
  1780.4 84.3 %collective-permute-done.5 = f32[1024,1024]{1,0:T(8,128)S(1)} collective-permute-done((f32[1024,1024]{1,0:T(8,128)S(1)}, f32[1024,1024]{1,0:T(8,128)S(1)}, u32[]{:S(2)}, u32[]{:S(2)}) %collective-permute-start.5) | collective-permute-done | bytes 4194336 | tf_op jit(solution)/shard_map/ppermute | solution.py:45
  1864.7 90.0 %collective-permute-done.11 = f32[1024,1024]{1,0:T(8,128)} collective-permute-done((f32[1024,1024]{1,0:T(8,128)S(1)}, f32[1024,1024]{1,0:T(8,128)}, u32[]{:S(2)}, u32[]{:S(2)}) %collective-permute-start.11) | collective-permute-done | bytes 4194336 | tf_op jit(solution)/shard_map/ppermute | solution.py:45
  1954.7 89.9 %collective-permute-done.17 = f32[1024,1024]{1,0:T(8,128)} collective-permute-done((f32[1024,1024]{1,0:T(8,128)S(1)}, f32[1024,1024]{1,0:T(8,128)}, u32[]{:S(2)}, u32[]{:S(2)}) %collective-permute-start.17) | collective-permute-done | bytes 4194336 | tf_op jit(solution)/shard_map/ppermute | solution.py:45
  2044.6 18.7 fusion.367
  2071.2 5.8 multiply_reduce_fusion.13
  2079.7 5.8 fusion.24
  2087.7 8.9 fusion.18
  2096.6 10.9 fusion.140
  2107.5 3.9 fusion.31
  2111.4 10.8 fusion.139
  2122.3 7.4 fusion.29
  2129.7 10.8 fusion.138
  2140.4 10.8 fusion.137
  2162.2 173.1 %all-reduce.7.cloned.1.call-done = (f32[1024,1024]{1,0:T(8,128)}, f32[1024,1024]{1,0:T(8,128)}, f32[1024,1024]{1,0:T(8,128)}, f32[1024,1024]{1,0:T(8,128)}) async-done(((f32[1024,1024]{1,0:T(8,128)}, f32[1024,1024]{1,0:T(8,128)}, f32[1024,1024]{1,0:T(8,128)}, f32[1024,1024]{1,0:T(8,128)}), (f32[1024,1024]{1,0:T(8,128)}, f32[1024,1024]{1,0:T(8,128)}, f32[1024,1024]{1,0:T(8,128)}, ...) | async-done | bytes 16777232 | tf_op jit(solution)/shard_map/psum | solution.py:148
  2335.3 7.9 fusion.366
  2346.1 3.5 convolution_convert_fusion
  2354.6 5.9 fusion.365
  2363.4 3.5 convolution_convert_fusion.1
  2372.0 5.9 fusion.364
  2380.7 3.5 convolution_convert_fusion.2
  2384.3 3.7 multiply_reduce_fusion.7
  2389.3 5.9 fusion.363
  2398.1 3.5 convolution_convert_fusion.3
  2419.1 29.7 %all-reduce.8 = (bf16[1024,32]{0,1:T(8,128)(2,1)}, bf16[1024,32]{0,1:T(8,128)(2,1)}, bf16[1024,32]{0,1:T(8,128)(2,1)}, bf16[1024,32]{0,1:T(8,128)(2,1)}) all-reduce(f32[1024,32]{0,1:T(8,128)S(1)} %maximum_multiply_fusion.3, f32[1024,32]{0,1:T(8,128)} %maximum_multiply_fusion.2, ...), channel_id=1, replica_groups=mesh['dp'=16,'head'=8] {'head'}, use_global_device_ids=true, to_apply=%region_65.67 | all-reduce | flops 131072 | bytes 786432 | tf_op jit(solution)/shard_map/psum | solution.py:203
  2456.1 10.8 all_to_all.6
  2469.0 12.5 all-reduce
  2486.1 64.2 %reduce-scatter.8.cloned.1.call-done = f32[2,16,8]{1,2,0:T(8,128)} async-done(((f32[2,16,128]{1,2,0:T(8,128)}), f32[2,16,8]{1,2,0:T(8,128)}) %reduce-scatter.8.cloned.1.call-update) | async-done | bytes 1040 | tf_op jit(solution)/shard_map/reduce_scatter | solution.py:333
  2551.6 73.9 %reduce-scatter.10.cloned.1.call-done = f32[64,32]{1,0:T(8,128)} async-done(((f32[1024,32]{1,0:T(8,128)}), f32[64,32]{1,0:T(8,128)}) %reduce-scatter.10.cloned.1.call-update) | async-done | bytes 8208
  2627.8 66.1 %all-reduce.1 = (f32[]{:T(128)}, f32[2,2]{0,1:T(2,128)S(1)}, f32[2,2]{0,1:T(2,128)S(1)}) all-reduce(f32[]{:T(128)S(6)} %div.320, f32[2,2]{0,1:T(2,128)S(1)} %pad_maximum_fusion.2, f32[2,2]{0,1:T(2,128)S(1)} %maximum_multiply_fusion.8), channel_id=1, replica_groups=mesh['dp'=16,'head'=8] {'dp','head'}, use_global_device_ids=true, to_apply=%region_37.39 | all-reduce | flops 9 | bytes 72 | tf_op jit(solution)/shard_map/psum | solution.py:360
  (678 shorter events, 243.1 us)
Async XLA Ops:
  7.2 1034.7 %copy-start = (bf16[512,1024]{1,0:T(8,128)(2,1)S(1)}, bf16[512,1024]{1,0:T(8,128)(2,1)}, u32[]{:S(2)}) copy-start(bf16[512,1024]{1,0:T(8,128)(2,1)} %param.31) | copy-start | bytes 3145732
  7.2 20.9 copy-start.1
  7.2 410.2 %reduce-scatter.6.cloned.1.call-start = ((), (), s32[]{:S(2)}) async-start(), calls=%async_computation.4 | async-start | bytes 17825792 | tf_op jit(solution)/shard_map/reduce_scatter | solution.py:285
  301.6 172.0 %all-gather.2.cloned.1.call-start = ((), (), s32[]{:S(2)}) async-start(), calls=%async_computation.5 | async-start | bytes 9437184 | tf_op jit(solution)/shard_map/all_gather | solution.py:296
  417.5 1917.8 %all-reduce.7.cloned.1.call-start = ((), (), s32[]{:S(2)}) async-start(), calls=%async_computation.8 | async-start | bytes 33554432 | tf_op jit(solution)/shard_map/psum | solution.py:148
  419.1 153.0 %copy-start.92 = (bf16[2,16,128]{2,1,0:T(8,128)(2,1)}, bf16[2,16,128]{2,1,0:T(8,128)(2,1)S(1)}, u32[]{:S(2)}) copy-start(bf16[2,16,128]{2,1,0:T(8,128)(2,1)S(1)} %convert_element_type.351) | copy-start | bytes 24580
  420.4 134.3 %copy-start.116 = (pred[2,512]{1,0:T(4,128)(4,1)}, pred[2,512]{1,0:T(4,128)(4,1)S(1)}, u32[]{:S(2)}) copy-start(pred[2,512]{1,0:T(4,128)(4,1)S(1)} %get-tuple-element.120) | copy-start | bytes 3076
  499.2 15.1 copy-start.33
  516.8 15.0 copy-start.76
  518.5 8.3 copy-start.60
  536.0 41.8 %collective-permute-start.18 = (f32[1024,1024]{1,0:T(8,128)}, f32[1024,1024]{1,0:T(8,128)}, u32[]{:S(2)}, u32[]{:S(2)}) collective-permute-start(f32[1024,1024]{1,0:T(8,128)} %fusion.400), channel_id=1, source_target_pairs={{0,1},{1,0},{2,3},{3,2},{4,5},{5,4},{6,7},{7,6},{8,9},{9,8},{10,11... | collective-permute-start | bytes 12582920 | tf_op jit(solution)/shard_map/ppermute | solution.py:45
  539.0 8.3 copy-start.56
  561.6 21.8 collective-permute-start
  571.0 17.3 collective-permute-start.6
  577.5 16.4 collective-permute-start.12
  582.2 92.0 %collective-permute-start.19 = (f32[1024,1024]{1,0:T(8,128)S(1)}, f32[1024,1024]{1,0:T(8,128)S(1)}, u32[]{:S(2)}, u32[]{:S(2)}) collective-permute-start(f32[1024,1024]{1,0:T(8,128)S(1)} %add.500), channel_id=1, source_target_pairs={{0,2},{1,3},{2,0},{3,1},{4,6},{5,7},{6,4},{7,5},{8,10},{9,11},{10,... | collective-permute-start | bytes 12582920 | tf_op jit(solution)/shard_map/ppermute | solution.py:45
  587.8 176.4 %collective-permute-start.1 = (f32[1024,1024]{1,0:T(8,128)S(1)}, f32[1024,1024]{1,0:T(8,128)}, u32[]{:S(2)}, u32[]{:S(2)}) collective-permute-start(f32[1024,1024]{1,0:T(8,128)S(1)} %add.448), channel_id=1, source_target_pairs={{0,2},{1,3},{2,0},{3,1},{4,6},{5,7},{6,4},{7,5},{8,10},{9,11},{10,... | collective-permute-start | bytes 12582920 | tf_op jit(solution)/shard_map/ppermute | solution.py:45
  592.7 261.4 %collective-permute-start.7 = (f32[1024,1024]{1,0:T(8,128)S(1)}, f32[1024,1024]{1,0:T(8,128)}, u32[]{:S(2)}, u32[]{:S(2)}) collective-permute-start(f32[1024,1024]{1,0:T(8,128)S(1)} %add.468), channel_id=1, source_target_pairs={{0,2},{1,3},{2,0},{3,1},{4,6},{5,7},{6,4},{7,5},{8,10},{9,11},{10,... | collective-permute-start | bytes 12582920 | tf_op jit(solution)/shard_map/ppermute | solution.py:45
  594.8 349.1 %collective-permute-start.13 = (f32[1024,1024]{1,0:T(8,128)S(1)}, f32[1024,1024]{1,0:T(8,128)}, u32[]{:S(2)}, u32[]{:S(2)}) collective-permute-start(f32[1024,1024]{1,0:T(8,128)S(1)} %add.484), channel_id=1, source_target_pairs={{0,2},{1,3},{2,0},{3,1},{4,6},{5,7},{6,4},{7,5},{8,10},{9,11},{10,... | collective-permute-start | bytes 12582920 | tf_op jit(solution)/shard_map/ppermute | solution.py:45
  675.1 360.1 %collective-permute-start.20 = (f32[1024,1024]{1,0:T(8,128)S(1)}, f32[1024,1024]{1,0:T(8,128)}, u32[]{:S(2)}, u32[]{:S(2)}) collective-permute-start(f32[1024,1024]{1,0:T(8,128)S(1)} %add.501), channel_id=1, source_target_pairs={{0,4},{1,5},{2,6},{3,7},{4,0},{5,1},{6,2},{7,3},{8,12},{9,13},{10,... | collective-permute-start | bytes 12582920 | tf_op jit(solution)/shard_map/ppermute | solution.py:45
  769.4 355.8 %collective-permute-start.2 = (f32[1024,1024]{1,0:T(8,128)}, f32[1024,1024]{1,0:T(8,128)}, u32[]{:S(2)}, u32[]{:S(2)}) collective-permute-start(f32[1024,1024]{1,0:T(8,128)} %add.449), channel_id=1, source_target_pairs={{0,4},{1,5},{2,6},{3,7},{4,0},{5,1},{6,2},{7,3},{8,12},{9,13},{10,... | collective-permute-start | bytes 12582920 | tf_op jit(solution)/shard_map/ppermute | solution.py:45
  857.2 357.8 %collective-permute-start.8 = (f32[1024,1024]{1,0:T(8,128)S(1)}, f32[1024,1024]{1,0:T(8,128)}, u32[]{:S(2)}, u32[]{:S(2)}) collective-permute-start(f32[1024,1024]{1,0:T(8,128)S(1)} %add.469), channel_id=1, source_target_pairs={{0,4},{1,5},{2,6},{3,7},{4,0},{5,1},{6,2},{7,3},{8,12},{9,13},{10,... | collective-permute-start | bytes 12582920 | tf_op jit(solution)/shard_map/ppermute | solution.py:45
  943.9 91.3 %copy-start.34 = (f32[2,512,1024]{2,1,0:T(8,128)S(1)}, f32[2,512,1024]{2,1,0:T(8,128)}, u32[]{:S(2)}) copy-start(f32[2,512,1024]{2,1,0:T(8,128)} %copy-done.33) | copy-start | bytes 12582916
  947.2 357.7 %collective-permute-start.14 = (f32[1024,1024]{1,0:T(8,128)S(1)}, f32[1024,1024]{1,0:T(8,128)}, u32[]{:S(2)}, u32[]{:S(2)}) collective-permute-start(f32[1024,1024]{1,0:T(8,128)S(1)} %add.485), channel_id=1, source_target_pairs={{0,4},{1,5},{2,6},{3,7},{4,0},{5,1},{6,2},{7,3},{8,12},{9,13},{10,... | collective-permute-start | bytes 12582920 | tf_op jit(solution)/shard_map/ppermute | solution.py:45
  1038.4 736.5 %copy-start.16 = (f32[1024,1024]{1,0:T(8,128)}, f32[1024,1024]{1,0:T(8,128)S(1)}, u32[]{:S(2)}) copy-start(f32[1024,1024]{1,0:T(8,128)S(1)} %get-tuple-element.69) | copy-start | bytes 12582916
  1041.9 83.3 %copy-start.32 = (f32[2,512,1024]{2,1,0:T(8,128)S(1)}, f32[2,512,1024]{2,1,0:T(8,128)}, u32[]{:S(2)}) copy-start(f32[2,512,1024]{2,1,0:T(8,128)} %get-tuple-element.70) | copy-start | bytes 12582916
  1048.6 269.3 %collective-permute-start.21 = (f32[1024,1024]{1,0:T(8,128)}, f32[1024,1024]{1,0:T(8,128)}, u32[]{:S(2)}, u32[]{:S(2)}) collective-permute-start(f32[1024,1024]{1,0:T(8,128)} %fusion.136), channel_id=1, source_target_pairs={{0,1},{1,0},{2,3},{3,2},{4,5},{5,4},{6,7},{7,6},{8,9},{9,8},{10,11... | collective-permute-start | bytes 12582920 | tf_op jit(solution)/shard_map/ppermute | solution.py:45
  1132.7 82.3 %copy-start.30 = (f32[2,512,1024]{2,1,0:T(8,128)S(1)}, f32[2,512,1024]{2,1,0:T(8,128)}, u32[]{:S(2)}) copy-start(f32[2,512,1024]{2,1,0:T(8,128)} %get-tuple-element.73) | copy-start | bytes 12582916
  1139.4 183.5 %collective-permute-start.3 = (f32[1024,1024]{1,0:T(8,128)}, f32[1024,1024]{1,0:T(8,128)}, u32[]{:S(2)}, u32[]{:S(2)}) collective-permute-start(f32[1024,1024]{1,0:T(8,128)} %fusion.133), channel_id=1, source_target_pairs={{0,1},{1,0},{2,3},{3,2},{4,5},{5,4},{6,7},{7,6},{8,9},{9,8},{10,11... | collective-permute-start | bytes 12582920 | tf_op jit(solution)/shard_map/ppermute | solution.py:45
  1221.6 83.3 %copy-start.29 = (f32[2,512,1024]{2,1,0:T(8,128)S(1)}, f32[2,512,1024]{2,1,0:T(8,128)}, u32[]{:S(2)}) copy-start(f32[2,512,1024]{2,1,0:T(8,128)} %get-tuple-element.72) | copy-start | bytes 12582916
  1226.9 101.6 %collective-permute-start.9 = (f32[1024,1024]{1,0:T(8,128)S(1)}, f32[1024,1024]{1,0:T(8,128)}, u32[]{:S(2)}, u32[]{:S(2)}) collective-permute-start(f32[1024,1024]{1,0:T(8,128)S(1)} %fusion.134), channel_id=1, source_target_pairs={{0,1},{1,0},{2,3},{3,2},{4,5},{5,4},{6,7},{7,6},{8,9},{9,8},{10,11... | collective-permute-start | bytes 12582920 | tf_op jit(solution)/shard_map/ppermute | solution.py:45
  1316.8 15.4 collective-permute-start.15
  1322.3 92.4 %collective-permute-start.22 = (f32[1024,1024]{1,0:T(8,128)S(1)}, f32[1024,1024]{1,0:T(8,128)}, u32[]{:S(2)}, u32[]{:S(2)}) collective-permute-start(f32[1024,1024]{1,0:T(8,128)S(1)} %add.506), channel_id=1, source_target_pairs={{0,2},{1,3},{2,0},{3,1},{4,6},{5,7},{6,4},{7,5},{8,10},{9,11},{10,... | collective-permute-start | bytes 12582920 | tf_op jit(solution)/shard_map/ppermute | solution.py:45
  1327.2 177.3 %collective-permute-start.4 = (f32[1024,1024]{1,0:T(8,128)S(1)}, f32[1024,1024]{1,0:T(8,128)}, u32[]{:S(2)}, u32[]{:S(2)}) collective-permute-start(f32[1024,1024]{1,0:T(8,128)S(1)} %add.456), channel_id=1, source_target_pairs={{0,2},{1,3},{2,0},{3,1},{4,6},{5,7},{6,4},{7,5},{8,10},{9,11},{10,... | collective-permute-start | bytes 12582920 | tf_op jit(solution)/shard_map/ppermute | solution.py:45
  1331.7 262.8 %collective-permute-start.10 = (f32[1024,1024]{1,0:T(8,128)S(1)}, f32[1024,1024]{1,0:T(8,128)}, u32[]{:S(2)}, u32[]{:S(2)}) collective-permute-start(f32[1024,1024]{1,0:T(8,128)S(1)} %add.474), channel_id=1, source_target_pairs={{0,2},{1,3},{2,0},{3,1},{4,6},{5,7},{6,4},{7,5},{8,10},{9,11},{10,... | collective-permute-start | bytes 12582920 | tf_op jit(solution)/shard_map/ppermute | solution.py:45
  1335.3 349.1 %collective-permute-start.16 = (f32[1024,1024]{1,0:T(8,128)S(1)}, f32[1024,1024]{1,0:T(8,128)}, u32[]{:S(2)}, u32[]{:S(2)}) collective-permute-start(f32[1024,1024]{1,0:T(8,128)S(1)} %add.490), channel_id=1, source_target_pairs={{0,2},{1,3},{2,0},{3,1},{4,6},{5,7},{6,4},{7,5},{8,10},{9,11},{10,... | collective-permute-start | bytes 12582920 | tf_op jit(solution)/shard_map/ppermute | solution.py:45
  1417.8 357.1 %collective-permute-start.23 = (f32[1024,1024]{1,0:T(8,128)S(1)}, f32[1024,1024]{1,0:T(8,128)}, u32[]{:S(2)}, u32[]{:S(2)}) collective-permute-start(f32[1024,1024]{1,0:T(8,128)S(1)} %add.507), channel_id=1, source_target_pairs={{0,4},{1,5},{2,6},{3,7},{4,0},{5,1},{6,2},{7,3},{8,12},{9,13},{10,... | collective-permute-start | bytes 12582920 | tf_op jit(solution)/shard_map/ppermute | solution.py:45
  1507.7 89.9 %copy-start.45 = (f32[1024,1024]{1,0:T(8,128)}, f32[1024,1024]{1,0:T(8,128)S(1)}, u32[]{:S(2)}) copy-start(f32[1024,1024]{1,0:T(8,128)S(1)} %add.457) | copy-start | bytes 12582916
  1507.7 357.0 %collective-permute-start.5 = (f32[1024,1024]{1,0:T(8,128)S(1)}, f32[1024,1024]{1,0:T(8,128)S(1)}, u32[]{:S(2)}, u32[]{:S(2)}) collective-permute-start(f32[1024,1024]{1,0:T(8,128)S(1)} %add.457), channel_id=1, source_target_pairs={{0,4},{1,5},{2,6},{3,7},{4,0},{5,1},{6,2},{7,3},{8,12},{9,13},{10,... | collective-permute-start | bytes 12582920 | tf_op jit(solution)/shard_map/ppermute | solution.py:45
  1597.6 89.9 %copy-start.46 = (f32[1024,1024]{1,0:T(8,128)}, f32[1024,1024]{1,0:T(8,128)S(1)}, u32[]{:S(2)}) copy-start(f32[1024,1024]{1,0:T(8,128)S(1)} %add.475) | copy-start | bytes 12582916
  1597.6 91.4 %copy-start.158 = (s32[8]{0:T(128)S(1)}, s32[8]{0:T(128)}, u32[]{:S(2)}) copy-start(s32[8]{0:T(128)} %param.23) | copy-start | bytes 100
  1597.6 91.5 %copy-start.127 = (pred[8,512]{1,0:T(8,128)(4,1)S(1)}, pred[8,512]{1,0:T(8,128)(4,1)}, u32[]{:S(2)}) copy-start(pred[8,512]{1,0:T(8,128)(4,1)} %copy-done.126) | copy-start | bytes 12292
  1597.6 91.6 %copy-start.165 = (s32[8]{0:T(128)S(1)}, s32[8]{0:T(128)}, u32[]{:S(2)}) copy-start(s32[8]{0:T(128)} %param.24) | copy-start | bytes 100
  1597.6 357.1 %collective-permute-start.11 = (f32[1024,1024]{1,0:T(8,128)S(1)}, f32[1024,1024]{1,0:T(8,128)}, u32[]{:S(2)}, u32[]{:S(2)}) collective-permute-start(f32[1024,1024]{1,0:T(8,128)S(1)} %add.475), channel_id=1, source_target_pairs={{0,4},{1,5},{2,6},{3,7},{4,0},{5,1},{6,2},{7,3},{8,12},{9,13},{10,... | collective-permute-start | bytes 12582920 | tf_op jit(solution)/shard_map/ppermute | solution.py:45
  1687.5 91.0 %copy-start.47 = (f32[1024,1024]{1,0:T(8,128)}, f32[1024,1024]{1,0:T(8,128)S(1)}, u32[]{:S(2)}) copy-start(f32[1024,1024]{1,0:T(8,128)S(1)} %add.491) | copy-start | bytes 12582916
  1687.5 357.1 %collective-permute-start.17 = (f32[1024,1024]{1,0:T(8,128)S(1)}, f32[1024,1024]{1,0:T(8,128)}, u32[]{:S(2)}, u32[]{:S(2)}) collective-permute-start(f32[1024,1024]{1,0:T(8,128)S(1)} %add.491), channel_id=1, source_target_pairs={{0,4},{1,5},{2,6},{3,7},{4,0},{5,1},{6,2},{7,3},{8,12},{9,13},{10,... | collective-permute-start | bytes 12582920 | tf_op jit(solution)/shard_map/ppermute | solution.py:45
  1864.7 90.0 %copy-start.53 = (f32[1024,1024]{1,0:T(8,128)}, f32[1024,1024]{1,0:T(8,128)S(1)}, u32[]{:S(2)}) copy-start(f32[1024,1024]{1,0:T(8,128)S(1)} %collective-permute-done.5) | copy-start | bytes 12582916
  2071.2 8.5 copy-start.9
  2151.3 398.9 %reduce-scatter.8.cloned.1.call-start = ((), (), s32[]{:S(2)}) async-start(), calls=%async_computation.6 | async-start | bytes 139264 | tf_op jit(solution)/shard_map/reduce_scatter | solution.py:333
  2335.3 7.9 copy-start.17
  2335.3 7.9 copy-start.55
  2349.6 53.7 %copy-start.82 = (bf16[2,2,64,512]{3,2,1,0:T(8,128)(2,1)}, bf16[2,2,64,512]{3,2,1,0:T(8,128)(2,1)S(1)}, u32[]{:S(2)}) copy-start(bf16[2,2,64,512]{3,2,1,0:T(8,128)(2,1)S(1)} %convolution_convert_fusion) | copy-start | bytes 786436
  2366.9 40.5 %copy-start.84 = (bf16[2,2,64,512]{3,2,1,0:T(8,128)(2,1)}, bf16[2,2,64,512]{3,2,1,0:T(8,128)(2,1)S(1)}, u32[]{:S(2)}) copy-start(bf16[2,2,64,512]{3,2,1,0:T(8,128)(2,1)S(1)} %convolution_convert_fusion.1) | copy-start | bytes 786436
  2384.3 27.4 %copy-start.86 = (bf16[2,2,64,512]{3,2,1,0:T(8,128)(2,1)}, bf16[2,2,64,512]{3,2,1,0:T(8,128)(2,1)S(1)}, u32[]{:S(2)}) copy-start(bf16[2,2,64,512]{3,2,1,0:T(8,128)(2,1)S(1)} %convolution_convert_fusion.2) | copy-start | bytes 786436
  2401.6 13.8 copy-start.88
  2418.3 32.7 %copy-start.43 = (bf16[2,512,1024]{2,1,0:T(8,128)(2,1)S(1)}, bf16[2,512,1024]{2,1,0:T(8,128)(2,1)}, u32[]{:S(2)}) copy-start(bf16[2,512,1024]{2,1,0:T(8,128)(2,1)} %get-tuple-element.76) | copy-start | bytes 6291460
  2482.5 143.0 %reduce-scatter.10.cloned.1.call-start = ((), (), s32[]{:S(2)}) async-start(), calls=%async_computation.7 | async-start | bytes 557056
  2482.5 67.7 %copy-start.128 = (f32[2,16,8]{1,2,0:T(8,128)S(1)}, f32[2,16,8]{1,2,0:T(8,128)}, u32[]{:S(2)}) copy-start(f32[2,16,8]{1,2,0:T(8,128)} %copy.338) | copy-start | bytes 3076
  2482.5 67.7 %copy-start.162 = (f32[2,16,8]{1,2,0:T(8,128)S(1)}, f32[2,16,8]{1,2,0:T(8,128)}, u32[]{:S(2)}) copy-start(f32[2,16,8]{1,2,0:T(8,128)} %param.42) | copy-start | bytes 3076
  2482.6 67.7 %copy-start.163 = (f32[2,16,8]{1,2,0:T(8,128)S(1)}, f32[2,16,8]{1,2,0:T(8,128)}, u32[]{:S(2)}) copy-start(f32[2,16,8]{1,2,0:T(8,128)} %param.40) | copy-start | bytes 3076
  2482.6 67.7 %copy-start.164 = (f32[2,16,8]{1,2,0:T(8,128)S(1)}, f32[2,16,8]{1,2,0:T(8,128)}, u32[]{:S(2)}) copy-start(f32[2,16,8]{1,2,0:T(8,128)} %param.39) | copy-start | bytes 3076
  2484.1 142.3 %copy-start.154 = (f32[2,64,16]{1,2,0:T(8,128)S(1)}, f32[2,64,16]{1,2,0:T(8,128)}, u32[]{:S(2)}) copy-start(f32[2,64,16]{1,2,0:T(8,128)} %param.41) | copy-start | bytes 24580
  2484.1 142.3 %copy-start.155 = (f32[2,64,16]{1,2,0:T(8,128)S(1)}, f32[2,64,16]{1,2,0:T(8,128)}, u32[]{:S(2)}) copy-start(f32[2,64,16]{1,2,0:T(8,128)} %param.38) | copy-start | bytes 24580
  2484.1 142.3 %copy-start.156 = (f32[2,64,16]{1,2,0:T(8,128)S(1)}, f32[2,64,16]{1,2,0:T(8,128)}, u32[]{:S(2)}) copy-start(f32[2,64,16]{1,2,0:T(8,128)} %param.37) | copy-start | bytes 24580
  (141 other events, 358.3 us)
Sparse Core Ops, SparseCore 0:
  301.7 115.6 reduce-scatter.5
  419.1 54.5 all-gather.1
  2151.4 183.7 all-reduce.6
  2482.6 67.5 reduce-scatter.7
  2553.6 71.8 reduce-scatter.9
